TPU v7x, 32 devices: a whole 2x2x4 slice. The times are simulated.
32 devices in a mesh: rep: 4 (over x, core), fsdp: 8 (over z, y).
Axes of the slice: x: 2, y: 2, z: 4, core: 2. Of those that a mesh axis runs over, the one named last changes fastest.
Arguments:
- tokens: bfloat16 [64, 512, 1024], P('rep', 'fsdp'), may hold values from -6 to 6
- cotangent: bfloat16 [64, 512, 1024], P('rep', 'fsdp'), may hold values from -6 to 6
- lengths: int32 [4, 16], P('rep'), may hold values from 1 to 512, as said below
- deal: int32 [4, 16], P('rep'), may hold values from 0 to 15, each once within a row
- norm_gain: bfloat16 [1024], P('fsdp'), may hold values from 0.099609375 to 1.8984375
- in_weight: bfloat16 [1024, 3072], P('fsdp'), may hold values from -0.1875 to 0.1875
- conv_weight: bfloat16 [1024, 3], P('fsdp'), may hold values from -3 to 3
- out_weight: bfloat16 [1024, 1024], P('fsdp'), may hold values from -0.1875 to 0.1875
- ffn_gain: bfloat16 [1024], P('fsdp'), may hold values from 0.099609375 to 1.8984375
- gate_weight: bfloat16 [1024, 4608], P('fsdp'), may hold values from -0.1875 to 0.1875
- up_weight: bfloat16 [1024, 4608], P('fsdp'), may hold values from -0.1875 to 0.1875
- down_weight: bfloat16 [4608, 1024], P('fsdp'), may hold values from -0.1875 to 0.1875
Outputs:
- block_out: bfloat16 [64, 512, 1024], P('rep', 'fsdp')
- block_grad: bfloat16 [64, 512, 1024], P('rep', 'fsdp')
- norm_gain_grad: float32 [1024], P('fsdp')
- in_grad: float32 [1024, 3072], P('fsdp')
- conv_grad: float32 [1024, 3], P('fsdp')
- out_grad: float32 [1024, 1024], P('fsdp')
- ffn_gain_grad: float32 [1024], P('fsdp')
- gate_grad: float32 [1024, 4608], P('fsdp')
- up_grad: float32 [1024, 4608], P('fsdp')
- down_grad: float32 [4608, 1024], P('fsdp')
Inputs may be any that keep to these rules, and one draw needn't show every extreme that they name: In each row, the 2 lengths of slots 2 i to 2 i + 1 sum to at most 768; in each row one such set sums to exactly 768 and holds a length of exactly 512. `deal`: each row is a permutation of the group's sequence numbers.
All inputs are finite; a program needn't handle non-finite values.
Results may differ from a plain program's by a relative error of at most 0.018.
Values may be sent and summed in bfloat16 or wider, within the bound.
A program may use at most 256 MiB of HBM per device.

v0:
```python
import jax
import jax.numpy as jnp
from jax import lax
from jax.sharding import PartitionSpec as P

SLOT = 512
CAP_DEV = 768
EPS = 1e-05


def row_scale(values):
    return lax.rsqrt(jnp.mean(values * values, axis=-1, keepdims=True) + EPS)


def norm_back(grad_unit, unit_rows, scale_rows):
    return scale_rows * (
        grad_unit - unit_rows * jnp.mean(grad_unit * unit_rows, axis=-1, keepdims=True)
    )


def lag_rows(values, amount):
    return jnp.pad(values, ((amount, 0), (0, 0)))[: values.shape[0]]


def lead_rows(values, amount):
    return jnp.pad(values, ((0, amount), (0, 0)))[amount:]


def over_rows(left_side, right_side):
    return lax.dot_general(
        left_side, right_side, (((0,), (0,)), ((), ())), preferred_element_type=jnp.float32
    )


def over_cols(left_side, right_side):
    return lax.dot_general(
        left_side, right_side, (((1,), (1,)), ((), ())), preferred_element_type=jnp.float32
    )


def pack_tables(lengths):
    group_len = lengths[0]
    seq_dev = group_len.shape[0] // lax.axis_size("fsdp")
    own_len = lax.dynamic_slice_in_dim(group_len, lax.axis_index("fsdp") * seq_dev, seq_dev)
    seq_ends = jnp.cumsum(own_len)
    starts = seq_ends - own_len
    total_len = seq_ends[seq_dev - 1]
    slot_ids = jnp.arange(seq_dev, dtype=jnp.int32)
    row_ids = jnp.arange(CAP_DEV, dtype=jnp.int32)
    which_seq = jnp.minimum(
        jnp.sum((row_ids[:, None] >= seq_ends[None, :]).astype(jnp.int32), axis=1), seq_dev - 1
    )
    row_start = jnp.sum(
        jnp.where(which_seq[:, None] == slot_ids[None, :], starts[None, :], 0), axis=1
    )
    row_live = row_ids < total_len
    position = jnp.where(row_live, row_ids - row_start, 0)
    source = jnp.where(row_live, which_seq * SLOT + position, 0)
    lag_masks = (
        (position >= 1).astype(jnp.float32)[:, None],
        (position >= 2).astype(jnp.float32)[:, None],
    )
    cell_ids = jnp.arange(seq_dev * SLOT, dtype=jnp.int32)
    cell_pick = (cell_ids // SLOT)[:, None] == slot_ids[None, :]
    cell_pos = cell_ids % SLOT
    cell_len = jnp.sum(jnp.where(cell_pick, own_len[None, :], 0), axis=1)
    cell_start = jnp.sum(jnp.where(cell_pick, starts[None, :], 0), axis=1)
    cell_live = cell_pos < cell_len
    back_index = jnp.where(cell_live, cell_start + cell_pos, 0)
    return (source, row_live, lag_masks, back_index, cell_live)


def to_rows(slot_values, source):
    width = slot_values.shape[2]
    return jnp.take(slot_values.reshape(-1, width), source, axis=0).astype(jnp.float32)


def to_slots(packed_rows, back_index, cell_live, seq_dev):
    cells = jnp.where(cell_live[:, None], jnp.take(packed_rows, back_index, axis=0), 0.0)
    return cells.astype(jnp.bfloat16).reshape(seq_dev, SLOT, packed_rows.shape[1])


def to_sources(received, deal_row):
    slot_ids = jnp.arange(deal_row.shape[0], dtype=jnp.int32)
    inverse = jnp.sum(
        jnp.where(deal_row[None, :] == slot_ids[:, None], slot_ids[None, :], 0), axis=1
    )
    return jnp.take(received, inverse, axis=0)


def forward_pass(token_rows, mix_set, ffn_set, lag_masks):
    norm_gain, in_weight, conv_weight, out_weight = mix_set
    ffn_gain, gate_weight, up_weight, down_weight = ffn_set
    width = in_weight.shape[0]
    scale_one = row_scale(token_rows)
    unit_one = token_rows * scale_one
    normed_one = (unit_one * norm_gain.astype(jnp.float32)).astype(jnp.bfloat16)
    projected = jnp.dot(normed_one, in_weight, preferred_element_type=jnp.float32)
    b_gate = projected[:, :width]
    c_gate = projected[:, width : 2 * width]
    x_value = projected[:, 2 * width :]
    product = b_gate * x_value
    lag_one = lag_rows(product, 1) * lag_masks[0]
    lag_two = lag_rows(product, 2) * lag_masks[1]
    taps = conv_weight.astype(jnp.float32)
    convolved = taps[:, 0] * lag_two + taps[:, 1] * lag_one + taps[:, 2] * product
    gated = (c_gate * convolved).astype(jnp.bfloat16)
    middle = token_rows + jnp.dot(gated, out_weight, preferred_element_type=jnp.float32)
    scale_two = row_scale(middle)
    unit_two = middle * scale_two
    normed_two = (unit_two * ffn_gain.astype(jnp.float32)).astype(jnp.bfloat16)
    gate_lin = jnp.dot(normed_two, gate_weight, preferred_element_type=jnp.float32)
    up_lin = jnp.dot(normed_two, up_weight, preferred_element_type=jnp.float32)
    hidden = (jax.nn.silu(gate_lin) * up_lin).astype(jnp.bfloat16)
    output = middle + jnp.dot(hidden, down_weight, preferred_element_type=jnp.float32)
    return (
        scale_one,
        unit_one,
        normed_one,
        b_gate,
        c_gate,
        x_value,
        product,
        lag_one,
        lag_two,
        convolved,
        gated,
        scale_two,
        unit_two,
        normed_two,
        gate_lin,
        up_lin,
        hidden,
        output,
    )


def backward_pass(saved, mix_set, ffn_set, lag_masks, grad_out):
    (
        scale_one,
        unit_one,
        normed_one,
        b_gate,
        c_gate,
        x_value,
        product,
        lag_one,
        lag_two,
        convolved,
        gated,
        scale_two,
        unit_two,
        normed_two,
        gate_lin,
        up_lin,
        hidden,
        output,
    ) = saved
    norm_gain, in_weight, conv_weight, out_weight = mix_set
    ffn_gain, gate_weight, up_weight, down_weight = ffn_set
    grad_ffn = grad_out.astype(jnp.bfloat16)
    down_grad = over_rows(hidden, grad_ffn)
    grad_hidden = over_cols(grad_ffn, down_weight)
    sigma = jax.nn.sigmoid(gate_lin)
    grad_gate = (grad_hidden * up_lin * sigma * (1.0 + gate_lin * (1.0 - sigma))).astype(
        jnp.bfloat16
    )
    grad_up = (grad_hidden * gate_lin * sigma).astype(jnp.bfloat16)
    gate_grad = over_rows(normed_two, grad_gate)
    up_grad = over_rows(normed_two, grad_up)
    grad_normed_two = over_cols(grad_gate, gate_weight) + over_cols(grad_up, up_weight)
    ffn_gain_grad = jnp.sum(grad_normed_two * unit_two, axis=0)
    grad_middle = grad_out + norm_back(
        grad_normed_two * ffn_gain.astype(jnp.float32), unit_two, scale_two
    )
    grad_mixed = grad_middle.astype(jnp.bfloat16)
    out_grad = over_rows(gated, grad_mixed)
    grad_gated = over_cols(grad_mixed, out_weight)
    grad_c = grad_gated * convolved
    grad_conv = grad_gated * c_gate
    conv_grad = jnp.stack(
        [
            jnp.sum(grad_conv * lag_two, axis=0),
            jnp.sum(grad_conv * lag_one, axis=0),
            jnp.sum(grad_conv * product, axis=0),
        ],
        axis=1,
    )
    taps = conv_weight.astype(jnp.float32)
    grad_product = (
        taps[:, 2] * grad_conv
        + taps[:, 1] * lead_rows(grad_conv * lag_masks[0], 1)
        + taps[:, 0] * lead_rows(grad_conv * lag_masks[1], 2)
    )
    grad_projected = jnp.concatenate(
        [grad_product * x_value, grad_c, grad_product * b_gate], axis=1
    ).astype(jnp.bfloat16)
    in_grad = over_rows(normed_one, grad_projected)
    grad_normed_one = over_cols(grad_projected, in_weight)
    norm_gain_grad = jnp.sum(grad_normed_one * unit_one, axis=0)
    grad_tokens = grad_middle + norm_back(
        grad_normed_one * norm_gain.astype(jnp.float32), unit_one, scale_one
    )
    return (
        grad_tokens,
        (
            norm_gain_grad,
            in_grad,
            conv_grad,
            out_grad,
            ffn_gain_grad,
            gate_grad,
            up_grad,
            down_grad,
        ),
    )


def body(
    tokens,
    cotangent,
    lengths,
    deal,
    norm_gain,
    in_weight,
    conv_weight,
    out_weight,
    ffn_gain,
    gate_weight,
    up_weight,
    down_weight,
):
    source, row_live, lag_masks, back_index, cell_live = pack_tables(lengths)
    seq_dev = deal.shape[1] // lax.axis_size("fsdp")
    deal_row = deal[0]
    sent_tokens = jnp.take(tokens, deal_row, axis=0)
    sent_cot = jnp.take(cotangent, deal_row, axis=0)
    slot_tokens, slot_cot = (
        lax.all_to_all(sent_tokens, "fsdp", split_axis=0, concat_axis=1, tiled=True),
        lax.all_to_all(sent_cot, "fsdp", split_axis=0, concat_axis=1, tiled=True),
    )
    token_rows = to_rows(slot_tokens, source)
    cot_rows = jnp.where(row_live[:, None], to_rows(slot_cot, source), 0.0)
    mix_set = (
        lax.all_gather(norm_gain, "fsdp", axis=0, tiled=True),
        lax.all_gather(in_weight, "fsdp", axis=0, tiled=True),
        lax.all_gather(conv_weight, "fsdp", axis=0, tiled=True),
        lax.all_gather(out_weight, "fsdp", axis=0, tiled=True),
    )
    ffn_set = (
        lax.all_gather(ffn_gain, "fsdp", axis=0, tiled=True),
        lax.all_gather(gate_weight, "fsdp", axis=0, tiled=True),
        lax.all_gather(up_weight, "fsdp", axis=0, tiled=True),
        lax.all_gather(down_weight, "fsdp", axis=0, tiled=True),
    )
    saved = forward_pass(token_rows, mix_set, ffn_set, lag_masks)
    out_slots = to_slots(saved[-1], back_index, cell_live, seq_dev)
    out_back = lax.all_to_all(out_slots, "fsdp", split_axis=1, concat_axis=0, tiled=True)
    block_out = to_sources(out_back, deal_row)
    again_slots = lax.all_to_all(sent_tokens, "fsdp", split_axis=0, concat_axis=1, tiled=True)
    again_rows = to_rows(again_slots, source)
    mix_back = (
        lax.all_gather(norm_gain, "fsdp", axis=0, tiled=True),
        lax.all_gather(in_weight, "fsdp", axis=0, tiled=True),
        lax.all_gather(conv_weight, "fsdp", axis=0, tiled=True),
        lax.all_gather(out_weight, "fsdp", axis=0, tiled=True),
    )
    ffn_back = (
        lax.all_gather(ffn_gain, "fsdp", axis=0, tiled=True),
        lax.all_gather(gate_weight, "fsdp", axis=0, tiled=True),
        lax.all_gather(up_weight, "fsdp", axis=0, tiled=True),
        lax.all_gather(down_weight, "fsdp", axis=0, tiled=True),
    )
    saved_back = forward_pass(again_rows, mix_back, ffn_back, lag_masks)
    grad_rows, weight_grads = backward_pass(saved_back, mix_back, ffn_back, lag_masks, cot_rows)
    grad_slots = to_slots(grad_rows, back_index, cell_live, seq_dev)
    grad_back = lax.all_to_all(grad_slots, "fsdp", split_axis=1, concat_axis=0, tiled=True)
    block_grad = to_sources(grad_back, deal_row)
    shares = (
        lax.psum_scatter(
            weight_grads[0].astype(jnp.bfloat16), "fsdp", scatter_dimension=0, tiled=True
        ).astype(jnp.float32),
        lax.psum_scatter(
            weight_grads[1].astype(jnp.bfloat16), "fsdp", scatter_dimension=0, tiled=True
        ).astype(jnp.float32),
        lax.psum_scatter(
            weight_grads[2].astype(jnp.bfloat16), "fsdp", scatter_dimension=0, tiled=True
        ).astype(jnp.float32),
        lax.psum_scatter(
            weight_grads[3].astype(jnp.bfloat16), "fsdp", scatter_dimension=0, tiled=True
        ).astype(jnp.float32),
        lax.psum_scatter(
            weight_grads[4].astype(jnp.bfloat16), "fsdp", scatter_dimension=0, tiled=True
        ).astype(jnp.float32),
        lax.psum_scatter(
            weight_grads[5].astype(jnp.bfloat16), "fsdp", scatter_dimension=0, tiled=True
        ).astype(jnp.float32),
        lax.psum_scatter(
            weight_grads[6].astype(jnp.bfloat16), "fsdp", scatter_dimension=0, tiled=True
        ).astype(jnp.float32),
        lax.psum_scatter(
            weight_grads[7].astype(jnp.bfloat16), "fsdp", scatter_dimension=0, tiled=True
        ).astype(jnp.float32),
    )
    summed = (
        lax.psum(shares[0].astype(jnp.bfloat16), "rep").astype(jnp.float32),
        lax.psum(shares[1].astype(jnp.bfloat16), "rep").astype(jnp.float32),
        lax.psum(shares[2].astype(jnp.bfloat16), "rep").astype(jnp.float32),
        lax.psum(shares[3].astype(jnp.bfloat16), "rep").astype(jnp.float32),
        lax.psum(shares[4].astype(jnp.bfloat16), "rep").astype(jnp.float32),
        lax.psum(shares[5].astype(jnp.bfloat16), "rep").astype(jnp.float32),
        lax.psum(shares[6].astype(jnp.bfloat16), "rep").astype(jnp.float32),
        lax.psum(shares[7].astype(jnp.bfloat16), "rep").astype(jnp.float32),
    )
    return (
        block_out,
        block_grad,
        summed[0],
        summed[1],
        summed[2],
        summed[3],
        summed[4],
        summed[5],
        summed[6],
        summed[7],
    )


def solution(mesh):
    placed = (
        P("rep", "fsdp", None),
        P("rep", "fsdp", None),
        P("rep", None),
        P("rep", None),
        P("fsdp"),
        P("fsdp", None),
        P("fsdp", None),
        P("fsdp", None),
        P("fsdp"),
        P("fsdp", None),
        P("fsdp", None),
        P("fsdp", None),
    )
    return jax.shard_map(
        body,
        mesh=mesh,
        in_specs=placed,
        out_specs=(
            P("rep", "fsdp", None),
            P("rep", "fsdp", None),
            P("fsdp"),
            P("fsdp", None),
            P("fsdp", None),
            P("fsdp", None),
            P("fsdp"),
            P("fsdp", None),
            P("fsdp", None),
            P("fsdp", None),
        ),
        check_vma=False,
    )
```

profile of v0, /device:TPU:0, one launch (start us, length us, event | category | flops | bytes accessed | tf_op | source)
XLA Modules:
  0.0 1630.6 jit_solution(14455915364186069048)
XLA Ops:
  10.6 2.0 gather_fusion.4
  12.6 3.7 gather_fusion
  16.4 3.3 broadcast_select_fusion.2
  19.7 92.7 %all_to_all.71 = bf16[16,64,1024]{2,1,0:T(8,128)(2,1)} all-to-all(bf16[16,64,1024]{2,1,0:T(8,128)(2,1)S(1)} %get-tuple-element.59), channel_id=1, replica_groups=mesh['rep'=4,'fsdp'=8] {'fsdp'}, dimensions={0} | all-to-all | bytes 4194304 | tf_op jit(solution)/shard_map/all_to_all | solution.py:239
  112.5 5.1 all-to-all-start.2
  119.0 68.1 %all-gather = bf16[8,1,128]{2,1,0:T(2,128)(2,1)S(1)} all-gather(bf16[1,1,128]{2,1,0:T(2,128)(2,1)S(1)} %bitcast.88), channel_id=1, replica_groups=mesh['rep'=4,'fsdp'=8] {'fsdp'}, dimensions={0}, use_global_device_ids=true | all-gather | bytes 2304 | tf_op jit(solution)/shard_map/all_gather | solution.py:245
  187.1 30.4 %all-gather.1 = bf16[8,1,128]{2,1,0:T(2,128)(2,1)S(1)} all-gather(bf16[1,1,128]{2,1,0:T(2,128)(2,1)S(1)} %bitcast.89), channel_id=1, replica_groups=mesh['rep'=4,'fsdp'=8] {'fsdp'}, dimensions={0}, use_global_device_ids=true | all-gather | bytes 2304 | tf_op jit(solution)/shard_map/all_gather | solution.py:251
  217.5 16.5 %all_gather.34 = bf16[1024,3]{0,1:T(4,128)(2,1)S(1)} all-gather(bf16[128,3]{0,1:T(4,128)(2,1)S(1)} %copy-done.28), channel_id=1, replica_groups=mesh['rep'=4,'fsdp'=8] {'fsdp'}, dimensions={0}, use_global_device_ids=true | all-gather | bytes 6912 | tf_op jit(solution)/shard_map/all_gather | solution.py:247
  235.7 1.8 copy.38
  237.5 3.1 copy.42
  240.6 3.5 gather_fusion.1
  244.2 6.6 gather_fusion.5
  251.4 7.5 fusion.25
  259.9 2.7 copy-done.2
  263.5 3.0 multiply_convert_fusion.7
  266.5 4.1 multiply_reduce_fusion.5
  270.6 1.7 copy-done.8
  272.3 1.5 multiply_convert_fusion.6
  273.8 100.0 %all-gather.12.cloned.1.call-done = bf16[1024,4608]{1,0:T(8,128)(2,1)} async-done(((bf16[128,4608]{1,0:T(8,128)(2,1)}), bf16[1024,4608]{1,0:T(8,128)(2,1)}) %all-gather.12.cloned.1.call-update) | async-done | bytes 9437200 | tf_op jit(solution)/shard_map/all_gather | solution.py:252
  373.8 13.4 fusion.46
  387.1 125.0 %all-gather.14.cloned.1.call-done = bf16[1024,4608]{1,0:T(8,128)(2,1)} async-done(((bf16[128,4608]{1,0:T(8,128)(2,1)}), bf16[1024,4608]{1,0:T(8,128)(2,1)}) %all-gather.14.cloned.1.call-update) | async-done | bytes 9437200 | tf_op jit(solution)/shard_map/all_gather | solution.py:253
  512.1 13.7 fusion.47
  525.7 124.7 %all-gather.16.cloned.1.call-done = bf16[4608,1024]{1,0:T(8,128)(2,1)} async-done(((bf16[576,1024]{1,0:T(8,128)(2,1)}), bf16[4608,1024]{1,0:T(8,128)(2,1)}) %all-gather.16.cloned.1.call-update) | async-done | bytes 9437200 | tf_op jit(solution)/shard_map/all_gather | solution.py:254
  650.4 28.2 %multiply_convert_fusion = (bf16[768,4608]{1,0:T(8,128)(2,1)}, bf16[768,4608]{1,0:T(8,128)(2,1)}, bf16[768,4608]{1,0:T(8,128)(2,1)}) fusion(f32[768,4608]{1,0:T(8,128)} %fusion.46, f32[768,4608]{1,0:T(8,128)} %fusion.47, bf16[4608,1024]{1,0:T(8,128)(2,1)} %all-gather.16.cloned.1.call-done, pred[768]{0:T(1024)(128)(4,1)S(1)} %iota_compare_fusion.2, ...), kind=kOutput, calls=%fused_computation.8 | convolution fusion | flops 7307526144 | bytes 60556800 | tf_op jit(solution)/shard_map/dot_general | solution.py:36
  678.6 13.5 fusion.48
  692.1 11.2 multiply_reduce_fusion
  703.4 1.8 multiply_add_fusion
  705.2 1.6 copy-done.3
  706.8 3.2 convolution_convert_fusion.4
  710.1 10.1 multiply_reduce_fusion.3
  720.7 3.6 multiply_convert_fusion.5
  724.3 3.1 multiply_convert_fusion.3
  728.6 8.2 convolution_convert_fusion.3
  738.2 13.2 convolution_convert_fusion.2
  751.5 12.9 convolution_convert_fusion.1
  765.9 13.5 convolution_convert_fusion
  780.1 12.6 convolution_add_fusion.1
  792.7 5.3 gather_fusion.2
  798.1 10.0 fusion.17
  808.1 1.4 fusion.16
  809.5 5.3 gather_fusion.6
  814.8 3.4 fusion.4
  818.2 3.5 copy.39
  821.7 4.3 all-to-all-start.1
  826.1 3.5 copy.43
  829.5 54.8 %all-to-all-done.1 = bf16[2,512,1024]{2,0,1:T(2,128)(2,1)} async-done(((bf16[2,512,1024]{2,0,1:T(2,128)(2,1)}), bf16[2,512,1024]{2,0,1:T(2,128)(2,1)}, u32[]{:S(2)}, u32[]{:S(2)}) %all-to-all-start.1) | async-done | bytes 2097184 | tf_op jit(solution)/shard_map/all_to_all | solution.py:258
  884.4 3.6 all-to-all-start.3
  889.1 70.7 %reduce-scatter.9.cloned.1.call-done = bf16[128,3072]{1,0:T(8,128)(2,1)} async-done(((bf16[1024,3072]{1,0:T(8,128)(2,1)}), bf16[128,3072]{1,0:T(8,128)(2,1)}) %reduce-scatter.9.cloned.1.call-update) | async-done | bytes 786448 | tf_op jit(solution)/shard_map/reduce_scatter | solution.py:283
  959.8 164.2 %reduce-scatter.13.cloned.1.call-done = bf16[128,4608]{1,0:T(8,128)(2,1)} async-done(((bf16[1024,4608]{1,0:T(8,128)(2,1)}), bf16[128,4608]{1,0:T(8,128)(2,1)}) %reduce-scatter.13.cloned.1.call-update) | async-done | bytes 1179664 | tf_op jit(solution)/shard_map/reduce_scatter | solution.py:295
  1124.0 166.2 %reduce-scatter.15.cloned.1.call-done = bf16[128,4608]{1,0:T(8,128)(2,1)} async-done(((bf16[1024,4608]{1,0:T(8,128)(2,1)}), bf16[128,4608]{1,0:T(8,128)(2,1)}) %reduce-scatter.15.cloned.1.call-update) | async-done | bytes 1179664 | tf_op jit(solution)/shard_map/reduce_scatter | solution.py:298
  1290.2 166.0 %reduce-scatter.17.cloned.1.call-done = bf16[576,1024]{1,0:T(8,128)(2,1)} async-done(((bf16[4608,1024]{1,0:T(8,128)(2,1)}), bf16[576,1024]{1,0:T(8,128)(2,1)}) %reduce-scatter.17.cloned.1.call-update) | async-done | bytes 1179664 | tf_op jit(solution)/shard_map/reduce_scatter | solution.py:301
  1457.6 19.5 %all-reduce.6 = (bf16[1024]{0:T(1024)(128)(2,1)S(1)}, bf16[1024]{0:T(1024)(128)(2,1)S(1)}) all-reduce(bf16[1024]{0:T(1024)(128)(2,1)S(1)} %get-tuple-element.18, bf16[1024]{0:T(1024)(128)(2,1)S(1)} %get-tuple-element.13), channel_id=2, replica_groups=mesh['rep'=4,'fsdp'=8] {'fsdp'}, use_global_device_ids=true, to_apply=%region_11.15.clone | all-reduce | flops 2048 | bytes 8192
  1477.2 43.3 %reduce-scatter.19.cloned.1.call-done = bf16[128,3]{1,0:T(8,128)(2,1)} async-done(((bf16[1024,3]{1,0:T(8,128)(2,1)}), bf16[128,3]{1,0:T(8,128)(2,1)}) %reduce-scatter.19.cloned.1.call-update) | async-done | bytes 784
  1521.3 5.7 all-reduce.7
  1528.6 2.2 copy.40
  1530.8 1.5 copy.41
  1532.9 1.5 copy.45
  1535.3 2.0 gather_fusion.3
  1537.3 3.7 gather_fusion.7
  1541.0 4.0 broadcast_select_fusion
  1545.1 69.7 %all-reduce.11.cloned.1.call-done = (bf16[128,3072]{1,0:T(8,128)(2,1)}, bf16[128,1024]{1,0:T(8,128)(2,1)}, bf16[128,4608]{1,0:T(8,128)(2,1)}, bf16[128,4608]{1,0:T(8,128)(2,1)}, bf16[576,1024]{1,0:T(8,128)(2,1)}) async-done(((bf16[128,3072]{1,0:T(8,128)(2,1)}, bf16[128,1024]{1,0:T(8,128)(2,1)}, bf16[128,4608]{1,0:T(8,128)(2,1)}, bf16[128,4608]{1,0:T(8,128)(2,1)}, bf16[576,1024]{1,0:T(8,128)(2,1)}), ...) | async-done | bytes 4587536 | tf_op jit(solution)/shard_map/psum | solution.py:307
  1614.8 3.1 convert_element_type.174
  1617.8 1.6 convert_element_type.176
  1619.5 1.7 convert_element_type.178
  (142 shorter events, 22.1 us)
Async XLA Ops:
  7.2 3.4 copy-start
  7.2 3.4 copy-start.31
  7.2 244.2 %all-gather.8.cloned.1.call-start = ((), (), s32[]{:S(2)}) async-start(), calls=%async_computation.10 | async-start | bytes 7077888 | tf_op jit(solution)/shard_map/all_gather | solution.py:246
  7.9 258.6 %all-gather.10.cloned.1.call-start = ((), (), s32[]{:S(2)}) async-start(), calls=%async_computation.11 | async-start | bytes 2359296 | tf_op jit(solution)/shard_map/all_gather | solution.py:248
  8.7 365.1 %all-gather.12.cloned.1.call-start = ((), (), s32[]{:S(2)}) async-start(), calls=%async_computation.12 | async-start | bytes 10616832 | tf_op jit(solution)/shard_map/all_gather | solution.py:252
  9.4 502.7 %all-gather.14.cloned.1.call-start = ((), (), s32[]{:S(2)}) async-start(), calls=%async_computation.13 | async-start | bytes 10616832 | tf_op jit(solution)/shard_map/all_gather | solution.py:253
  10.0 640.4 %all-gather.16.cloned.1.call-start = ((), (), s32[]{:S(2)}) async-start(), calls=%async_computation.14 | async-start | bytes 10616832 | tf_op jit(solution)/shard_map/all_gather | solution.py:254
  12.6 3.8 copy-start.12
  112.4 5.2 copy-start.26
  112.5 6.5 copy-start.29
  112.5 74.6 %copy-start.30 = (bf16[128]{0:T(256)(128)(2,1)S(1)}, bf16[128]{0:T(256)(128)(2,1)}, u32[]{:S(2)}) copy-start(bf16[128]{0:T(256)(128)(2,1)} %param.26) | copy-start | bytes 772
  112.5 105.1 %copy-start.28 = (bf16[128,3]{0,1:T(4,128)(2,1)S(1)}, bf16[128,3]{0,1:T(4,128)(2,1)}, u32[]{:S(2)}) copy-start(bf16[128,3]{0,1:T(4,128)(2,1)} %param.24) | copy-start | bytes 2308
  112.5 125.0 %all-to-all-start.2 = ((bf16[16,64,1024]{2,1,0:T(8,128)(2,1)}), bf16[16,64,1024]{2,1,0:T(8,128)(2,1)}, u32[]{:S(2)}, u32[]{:S(2)}) async-start(bf16[16,64,1024]{2,1,0:T(8,128)(2,1)} %get-tuple-element.58), calls=%async_computation.2 | async-start | bytes 4194304 | tf_op jit(solution)/shard_map/all_to_all | solution.py:240
  117.6 771.5 %reduce-scatter.11.cloned.1.call-start = ((), (), s32[]{:S(2)}) async-start(), calls=%async_computation.16 | async-start | bytes 2359296 | tf_op jit(solution)/shard_map/reduce_scatter | solution.py:289
  234.9 0.8 copy-start.24
  244.2 6.6 copy-start.6
  259.0 3.7 copy-start.2
  259.9 3.6 copy-start.5
  270.6 1.7 copy-start.8
  678.6 13.5 copy-start.9
  678.6 13.5 copy-start.34
  692.1 11.3 copy-start.13
  703.4 3.4 copy-start.16
  705.2 1.6 copy-start.3
  710.0 249.8 %reduce-scatter.9.cloned.1.call-start = ((), (), s32[]{:S(2)}) async-start(), calls=%async_computation.15 | async-start | bytes 7077888 | tf_op jit(solution)/shard_map/reduce_scatter | solution.py:283
  720.2 7.3 copy-start.19
  724.3 3.1 copy-start.15
  727.4 1.1 copy-start.18
  736.8 1.4 copy-start.17
  736.8 387.2 %reduce-scatter.13.cloned.1.call-start = ((), (), s32[]{:S(2)}) async-start(), calls=%async_computation.17 | async-start | bytes 10616832 | tf_op jit(solution)/shard_map/reduce_scatter | solution.py:295
  751.5 538.7 %reduce-scatter.15.cloned.1.call-start = ((), (), s32[]{:S(2)}) async-start(), calls=%async_computation.18 | async-start | bytes 10616832 | tf_op jit(solution)/shard_map/reduce_scatter | solution.py:298
  764.5 1.4 copy-start.14
  764.5 691.7 %reduce-scatter.17.cloned.1.call-start = ((), (), s32[]{:S(2)}) async-start(), calls=%async_computation.19 | async-start | bytes 10616832 | tf_op jit(solution)/shard_map/reduce_scatter | solution.py:301
  779.3 0.7 copy-start.25
  779.3 0.7 copy-start.27
  798.1 10.0 copy-start.4
  798.1 10.0 copy-start.7
  821.7 62.7 %all-to-all-start.1 = ((bf16[2,512,1024]{2,0,1:T(2,128)(2,1)}), bf16[2,512,1024]{2,0,1:T(2,128)(2,1)}, u32[]{:S(2)}, u32[]{:S(2)}) async-start(bf16[2,512,1024]{2,0,1:T(2,128)(2,1)} %copy.39), calls=%async_computation.1 | async-start | bytes 4194304 | tf_op jit(solution)/shard_map/all_to_all | solution.py:258
  884.4 647.9 %all-to-all-start.3 = ((bf16[2,512,1024]{2,0,1:T(2,128)(2,1)}), bf16[2,512,1024]{2,0,1:T(2,128)(2,1)S(1)}, u32[]{:S(2)}, u32[]{:S(2)}) async-start(bf16[2,512,1024]{2,0,1:T(2,128)(2,1)} %copy.43), calls=%async_computation.3 | async-start | bytes 4194304 | tf_op jit(solution)/shard_map/all_to_all | solution.py:277
  888.0 568.2 %copy-start.33 = (u32[32]{0:T(128)S(1)}, u32[32]{0:T(128)}, u32[]{:S(2)}) copy-start(u32[32]{0:T(128)} %constant.108) | copy-start | bytes 388
  888.0 569.4 %copy-start.32 = (s32[1,16]{1,0:T(1,128)S(1)}, s32[1,16]{1,0:T(1,128)}, u32[]{:S(2)}) copy-start(s32[1,16]{1,0:T(1,128)} %param.21) | copy-start | bytes 196
  888.0 632.5 %reduce-scatter.19.cloned.1.call-start = ((), (), s32[]{:S(2)}) async-start(), calls=%async_computation.20 | async-start | bytes 294912
  889.0 725.7 %all-reduce.11.cloned.1.call-start = ((), (), s32[]{:S(2)}) async-start(), calls=%async_computation.21 | async-start | bytes 9175040 | tf_op jit(solution)/shard_map/psum | solution.py:307
  1532.9 2.4 copy-start.10
  1537.3 3.7 copy-start.11
  1614.8 3.1 copy-start.21
  1614.8 4.7 copy-start.20
  1617.8 3.3 copy-start.22
  1619.5 3.0 copy-start.23
  1619.5 3.8 copy-start.1
Sparse Core Ops, SparseCore 0:
  10.2 174.4 all-gather.7
  186.8 48.0 all-gather.9
  237.1 136.5 all-gather.11
  375.8 136.2 all-gather.13
  514.1 136.2 all-gather.15
  710.1 65.9 reduce-scatter.10
  779.7 180.0 reduce-scatter.8
  963.4 160.5 reduce-scatter.12
  1127.6 162.5 reduce-scatter.14
  1293.6 162.5 reduce-scatter.16
  1460.1 60.3 reduce-scatter.18
  1523.1 91.6 all-reduce.10
where the time goes:
time: 1640 us; the launch traced here: 1630 us
  waiting for transfers between devices  1090 us (66%)
  blocking collectives  233 us (14%)
  matrix products  175 us (11%)
  local copies, waits for them, and re-layouts  66 us (4%)
  other arithmetic  39.3 us (2%)
    reduce_scatter x1, waiting for transfers between devices, body(): lax.psum_scatter(weight_grads[6].astype(jnp.bfloat16), 'fsdp', scatter_di...  166 us
    reduce_scatter x1, waiting for transfers between devices, body(): lax.psum_scatter(weight_grads[7].astype(jnp.bfloat16), 'fsdp', scatter_di...  166 us
    reduce_scatter x1, waiting for transfers between devices, body(): lax.psum_scatter(weight_grads[5].astype(jnp.bfloat16), 'fsdp', scatter_di...  164 us
    all_gather x1, waiting for transfers between devices, body(): lax.all_gather(up_weight, 'fsdp', axis=0, tiled=True)  125 us
    all_gather x1, waiting for transfers between devices, body(): lax.all_gather(down_weight, 'fsdp', axis=0, tiled=True)  125 us
    all_gather x1, waiting for transfers between devices, body(): lax.all_gather(gate_weight, 'fsdp', axis=0, tiled=True)  100 us
    all_to_all x1, blocking collectives, body(): lax.all_to_all(sent_tokens, 'fsdp', split_axis=0, concat_axis=1, tiled=True)  92.7 us
    dot_general x5, matrix products, over_cols(): lax.dot_general(left_side, right_side, (((1,), (1,)), ((), ())), preferre...  73 us
  transfers between devices with their start and end apart: 15, of which 10 were waited for; matrix products, arithmetic and copies ran while one was open for 12% of the time, Pallas kernels for 0%

commit v1 on v0

--- a/solution.py
+++ b/solution.py
@@ -6,6 +6,18 @@
 SLOT = 512
 CAP_DEV = 768
 EPS = 1e-05
+
+
+def doubled_up(x, axis, dim):
+    ways, here = (lax.axis_size(axis), lax.axis_index(axis))
+    grown, reach = (x, 1)
+    while reach < ways:
+        theirs = lax.ppermute(grown, axis, [(d, d ^ reach) for d in range(ways)])
+        mine_first = jnp.concatenate([grown, theirs], axis=dim)
+        theirs_first = jnp.concatenate([theirs, grown], axis=dim)
+        grown = jnp.where(here & reach == 0, mine_first, theirs_first)
+        reach = 2 * reach
+    return grown
 
 
 def row_scale(values):
@@ -251,7 +263,7 @@
         lax.all_gather(ffn_gain, "fsdp", axis=0, tiled=True),
         lax.all_gather(gate_weight, "fsdp", axis=0, tiled=True),
         lax.all_gather(up_weight, "fsdp", axis=0, tiled=True),
-        lax.all_gather(down_weight, "fsdp", axis=0, tiled=True),
+        doubled_up(down_weight, "fsdp", 0),
     )
     saved = forward_pass(token_rows, mix_set, ffn_set, lag_masks)
     out_slots = to_slots(saved[-1], back_index, cell_live, seq_dev)

time: 1640 us -> 1840 us (1.12)
  waiting for transfers between devices: 1090 us -> 1270 us
    ppermute x0 -> x3, waiting for transfers between devices: none -> 412 us  [doubled_up(): theirs = lax.ppermute(grown, axis, [(d, d ^ reach) for d in range(ways)])]
    reduce_scatter x1, waiting for transfers between devices: 164 us -> 0.02 us  [body(): lax.psum_scatter(weight_grads[5].astype(jnp.bfloat16), 'fsdp', scatter_di...]
    reduce_scatter x1, waiting for transfers between devices: 70.7 us -> 0.02 us  [body(): lax.psum_scatter(weight_grads[1].astype(jnp.bfloat16), 'fsdp', scatter_di...]
    all_to_all x1, waiting for transfers between devices: 54.8 us -> 95.6 us  [body(): lax.all_to_all(out_slots, 'fsdp', split_axis=1, concat_axis=0, tiled=True)]
    reduce_scatter x1, waiting for transfers between devices: 166 us -> 134 us  [body(): lax.psum_scatter(weight_grads[6].astype(jnp.bfloat16), 'fsdp', scatter_di...]
  transfers between devices with their start and end apart: 15 -> 18, of which waited for: 10 -> 11; matrix products, arithmetic and copies ran while one was open for 12% -> 12% of each run, Pallas kernels for 0% -> 0%
where the time goes in v1:
time: 1840 us; the launch traced here: 1830 us
  waiting for transfers between devices  1270 us (69%)
  blocking collectives  233 us (13%)
  matrix products  177 us (10%)
  local copies, waits for them, and re-layouts  65.3 us (4%)
  other arithmetic  48.5 us (3%)
    ppermute x3, waiting for transfers between devices, doubled_up(): theirs = lax.ppermute(grown, axis, [(d, d ^ reach) for d in range(ways)])  412 us
    reduce_scatter x1, waiting for transfers between devices, body(): lax.psum_scatter(weight_grads[7].astype(jnp.bfloat16), 'fsdp', scatter_di...  166 us
    reduce_scatter x1, waiting for transfers between devices, body(): lax.psum_scatter(weight_grads[6].astype(jnp.bfloat16), 'fsdp', scatter_di...  134 us
    all_gather x1, waiting for transfers between devices, body(): lax.all_gather(up_weight, 'fsdp', axis=0, tiled=True)  125 us
    all_gather x1, waiting for transfers between devices, body(): lax.all_gather(down_weight, 'fsdp', axis=0, tiled=True)  124 us
    all_gather x1, waiting for transfers between devices, body(): lax.all_gather(gate_weight, 'fsdp', axis=0, tiled=True)  99.9 us
    all_to_all x1, waiting for transfers between devices, body(): lax.all_to_all(out_slots, 'fsdp', split_axis=1, concat_axis=0, tiled=True)  95.6 us
    all_to_all x1, blocking collectives, body(): lax.all_to_all(sent_tokens, 'fsdp', split_axis=0, concat_axis=1, tiled=True)  92.7 us
  transfers between devices with their start and end apart: 18, of which 11 were waited for; matrix products, arithmetic and copies ran while one was open for 12% of the time, Pallas kernels for 0%

profile of v1, /device:TPU:0, one launch (start us, length us, event | category | flops | bytes accessed | tf_op | source)
XLA Modules:
  0.0 1829.9 jit_solution(16258065482002926877)
XLA Ops:
  10.6 2.0 gather_fusion.4
  12.6 3.7 gather_fusion
  16.4 3.3 broadcast_select_fusion.2
  19.7 92.7 %all_to_all.71 = bf16[16,64,1024]{2,1,0:T(8,128)(2,1)} all-to-all(bf16[16,64,1024]{2,1,0:T(8,128)(2,1)S(1)} %get-tuple-element.59), channel_id=1, replica_groups=mesh['rep'=4,'fsdp'=8] {'fsdp'}, dimensions={0} | all-to-all | bytes 4194304 | tf_op jit(solution)/shard_map/all_to_all | solution.py:251
  112.5 5.1 all-to-all-start.2
  119.0 68.1 %all-gather = bf16[8,1,128]{2,1,0:T(2,128)(2,1)S(1)} all-gather(bf16[1,1,128]{2,1,0:T(2,128)(2,1)S(1)} %bitcast.87), channel_id=1, replica_groups=mesh['rep'=4,'fsdp'=8] {'fsdp'}, dimensions={0}, use_global_device_ids=true | all-gather | bytes 2304 | tf_op jit(solution)/shard_map/all_gather | solution.py:257
  187.1 30.4 %all-gather.1 = bf16[8,1,128]{2,1,0:T(2,128)(2,1)S(1)} all-gather(bf16[1,1,128]{2,1,0:T(2,128)(2,1)S(1)} %bitcast.88), channel_id=1, replica_groups=mesh['rep'=4,'fsdp'=8] {'fsdp'}, dimensions={0}, use_global_device_ids=true | all-gather | bytes 2304 | tf_op jit(solution)/shard_map/all_gather | solution.py:263
  217.5 16.5 all_gather.33
  235.6 1.8 copy.38
  237.5 3.1 copy.42
  240.6 3.5 gather_fusion.1
  244.2 6.6 gather_fusion.5
  251.4 7.5 fusion.33
  259.9 2.7 copy-done.2
  263.5 3.0 multiply_convert_fusion.7
  266.5 4.1 multiply_reduce_fusion.5
  270.6 1.7 copy-done.8
  273.8 99.9 %all-gather.12.cloned.1.call-done = bf16[1024,4608]{1,0:T(8,128)(2,1)} async-done(((bf16[128,4608]{1,0:T(8,128)(2,1)}), bf16[1024,4608]{1,0:T(8,128)(2,1)}) %all-gather.12.cloned.1.call-update) | async-done | bytes 9437200 | tf_op jit(solution)/shard_map/all_gather | solution.py:264
  373.7 13.4 fusion.55
  387.1 125.0 %all-gather.14.cloned.1.call-done = bf16[1024,4608]{1,0:T(8,128)(2,1)} async-done(((bf16[128,4608]{1,0:T(8,128)(2,1)}), bf16[1024,4608]{1,0:T(8,128)(2,1)}) %all-gather.14.cloned.1.call-update) | async-done | bytes 9437200 | tf_op jit(solution)/shard_map/all_gather | solution.py:265
  512.1 13.9 fusion.56
  526.0 124.4 %all-gather.16.cloned.1.call-done = bf16[4608,1024]{1,0:T(8,128)(2,1)} async-done(((bf16[576,1024]{1,0:T(8,128)(2,1)}), bf16[4608,1024]{1,0:T(8,128)(2,1)}) %all-gather.16.cloned.1.call-update) | async-done | bytes 9437200 | tf_op jit(solution)/shard_map/all_gather | solution.py:284
  650.4 27.9 %multiply_convert_fusion = (bf16[768,4608]{1,0:T(8,128)(2,1)}, bf16[768,4608]{1,0:T(8,128)(2,1)}, bf16[768,4608]{1,0:T(8,128)(2,1)}) fusion(f32[768,4608]{1,0:T(8,128)} %fusion.55, f32[768,4608]{1,0:T(8,128)} %fusion.56, bf16[4608,1024]{1,0:T(8,128)(2,1)} %all-gather.16.cloned.1.call-done, pred[768]{0:T(1024)(128)(4,1)S(1)} %iota_compare_fusion.2, ...), kind=kOutput, calls=%fused_computation.8 | convolution fusion | flops 7307526144 | bytes 60556800 | tf_op jit(solution)/shard_map/dot_general | solution.py:48
  678.3 13.5 fusion.57
  691.8 11.2 multiply_reduce_fusion
  703.1 1.5 multiply_add_fusion
  704.7 1.6 copy-done.3
  706.3 3.2 convolution_convert_fusion.4
  709.5 10.1 multiply_reduce_fusion.3
  720.1 3.6 multiply_convert_fusion.5
  723.8 3.1 multiply_convert_fusion.3
  728.0 8.1 convolution_convert_fusion.3
  737.6 13.0 convolution_convert_fusion.2
  750.7 12.9 convolution_convert_fusion.1
  765.4 13.7 convolution_convert_fusion
  779.1 19.3 %collective-permute-done = bf16[576,1024]{1,0:T(8,128)(2,1)} collective-permute-done((bf16[576,1024]{1,0:T(8,128)(2,1)S(1)}, bf16[576,1024]{1,0:T(8,128)(2,1)}, u32[]{:S(2)}, u32[]{:S(2)}) %collective-permute-start) | collective-permute-done | bytes 1179680 | tf_op jit(solution)/shard_map/ppermute | solution.py:15
  798.4 3.3 maximum_select_fusion.3
  801.7 87.6 %collective-permute-done.1 = bf16[1152,1024]{1,0:T(8,128)(2,1)} collective-permute-done((bf16[1152,1024]{1,0:T(8,128)(2,1)}, bf16[1152,1024]{1,0:T(8,128)(2,1)}, u32[]{:S(2)}, u32[]{:S(2)}) %collective-permute-start.1) | collective-permute-done | bytes 2359328 | tf_op jit(solution)/shard_map/ppermute | solution.py:15
  889.3 6.3 maximum_select_fusion.2
  895.6 2.4 collective-permute-start.2
  898.1 304.9 %collective-permute-done.2 = bf16[2304,1024]{1,0:T(8,128)(2,1)} collective-permute-done((bf16[2304,1024]{1,0:T(8,128)(2,1)}, bf16[2304,1024]{1,0:T(8,128)(2,1)}, u32[]{:S(2)}, u32[]{:S(2)}) %collective-permute-start.2) | collective-permute-done | bytes 4718624 | tf_op jit(solution)/shard_map/ppermute | solution.py:15
  1203.0 14.1 fusion.28
  1217.1 5.3 gather_fusion.2
  1222.5 10.0 fusion.24
  1234.0 5.3 gather_fusion.6
  1239.4 3.0 fusion.11
  1242.4 3.5 copy.39
  1245.8 6.3 all-to-all-start.1
  1252.1 3.5 copy.43
  1255.6 95.6 %all-to-all-done.1 = bf16[2,512,1024]{2,0,1:T(2,128)(2,1)} async-done(((bf16[2,512,1024]{2,0,1:T(2,128)(2,1)}), bf16[2,512,1024]{2,0,1:T(2,128)(2,1)}, u32[]{:S(2)}, u32[]{:S(2)}) %all-to-all-start.1) | async-done | bytes 2097184 | tf_op jit(solution)/shard_map/all_to_all | solution.py:270
  1351.2 3.6 all-to-all-start.3
  1356.0 133.8 %reduce-scatter.15.cloned.1.call-done = bf16[128,4608]{1,0:T(8,128)(2,1)} async-done(((bf16[1024,4608]{1,0:T(8,128)(2,1)}), bf16[128,4608]{1,0:T(8,128)(2,1)}) %reduce-scatter.15.cloned.1.call-update) | async-done | bytes 1179664 | tf_op jit(solution)/shard_map/reduce_scatter | solution.py:310
  1489.8 166.0 %reduce-scatter.17.cloned.1.call-done = bf16[576,1024]{1,0:T(8,128)(2,1)} async-done(((bf16[4608,1024]{1,0:T(8,128)(2,1)}), bf16[576,1024]{1,0:T(8,128)(2,1)}) %reduce-scatter.17.cloned.1.call-update) | async-done | bytes 1179664 | tf_op jit(solution)/shard_map/reduce_scatter | solution.py:313
  1657.2 19.5 %all-reduce.6 = (bf16[1024]{0:T(1024)(128)(2,1)S(1)}, bf16[1024]{0:T(1024)(128)(2,1)S(1)}) all-reduce(bf16[1024]{0:T(1024)(128)(2,1)S(1)} %get-tuple-element.18, bf16[1024]{0:T(1024)(128)(2,1)S(1)} %get-tuple-element.13), channel_id=2, replica_groups=mesh['rep'=4,'fsdp'=8] {'fsdp'}, use_global_device_ids=true, to_apply=%region_11.15.clone | all-reduce | flops 2048 | bytes 8192
  1676.8 43.3 %reduce-scatter.19.cloned.1.call-done = bf16[128,3]{1,0:T(8,128)(2,1)} async-done(((bf16[1024,3]{1,0:T(8,128)(2,1)}), bf16[128,3]{1,0:T(8,128)(2,1)}) %reduce-scatter.19.cloned.1.call-update) | async-done | bytes 784
  1720.9 5.7 all-reduce.7
  1728.2 2.2 copy.40
  1734.9 2.0 gather_fusion.3
  1736.9 3.7 gather_fusion.7
  1740.6 4.0 broadcast_select_fusion
  1744.7 69.7 %all-reduce.11.cloned.1.call-done = (bf16[128,3072]{1,0:T(8,128)(2,1)}, bf16[128,1024]{1,0:T(8,128)(2,1)}, bf16[128,4608]{1,0:T(8,128)(2,1)}, bf16[128,4608]{1,0:T(8,128)(2,1)}, bf16[576,1024]{1,0:T(8,128)(2,1)}) async-done(((bf16[128,3072]{1,0:T(8,128)(2,1)}, bf16[128,1024]{1,0:T(8,128)(2,1)}, bf16[128,4608]{1,0:T(8,128)(2,1)}, bf16[128,4608]{1,0:T(8,128)(2,1)}, bf16[576,1024]{1,0:T(8,128)(2,1)}), ...) | async-done | bytes 4587536 | tf_op jit(solution)/shard_map/psum | solution.py:319
  1814.3 3.1 convert_element_type.174
  1817.4 1.6 convert_element_type.176
  1819.0 1.7 convert_element_type.178
  (152 shorter events, 27.9 us)
Async XLA Ops:
  7.2 3.4 copy-start
  7.2 3.4 copy-start.32
  7.2 244.2 %all-gather.8.cloned.1.call-start = ((), (), s32[]{:S(2)}) async-start(), calls=%async_computation.10 | async-start | bytes 7077888 | tf_op jit(solution)/shard_map/all_gather | solution.py:258
  7.9 258.6 %all-gather.10.cloned.1.call-start = ((), (), s32[]{:S(2)}) async-start(), calls=%async_computation.11 | async-start | bytes 2359296 | tf_op jit(solution)/shard_map/all_gather | solution.py:260
  8.7 365.1 %all-gather.12.cloned.1.call-start = ((), (), s32[]{:S(2)}) async-start(), calls=%async_computation.12 | async-start | bytes 10616832 | tf_op jit(solution)/shard_map/all_gather | solution.py:264
  9.4 502.6 %all-gather.14.cloned.1.call-start = ((), (), s32[]{:S(2)}) async-start(), calls=%async_computation.13 | async-start | bytes 10616832 | tf_op jit(solution)/shard_map/all_gather | solution.py:265
  10.0 640.4 %all-gather.16.cloned.1.call-start = ((), (), s32[]{:S(2)}) async-start(), calls=%async_computation.14 | async-start | bytes 10616832 | tf_op jit(solution)/shard_map/all_gather | solution.py:284
  12.6 3.8 copy-start.12
  112.4 5.2 copy-start.27
  112.5 6.5 copy-start.30
  112.5 74.6 %copy-start.31 = (bf16[128]{0:T(256)(128)(2,1)S(1)}, bf16[128]{0:T(256)(128)(2,1)}, u32[]{:S(2)}) copy-start(bf16[128]{0:T(256)(128)(2,1)} %param.26) | copy-start | bytes 772
  112.5 105.1 %copy-start.29 = (bf16[128,3]{0,1:T(4,128)(2,1)S(1)}, bf16[128,3]{0,1:T(4,128)(2,1)}, u32[]{:S(2)}) copy-start(bf16[128,3]{0,1:T(4,128)(2,1)} %param.24) | copy-start | bytes 2308
  112.5 125.0 %all-to-all-start.2 = ((bf16[16,64,1024]{2,1,0:T(8,128)(2,1)}), bf16[16,64,1024]{2,1,0:T(8,128)(2,1)}, u32[]{:S(2)}, u32[]{:S(2)}) async-start(bf16[16,64,1024]{2,1,0:T(8,128)(2,1)} %get-tuple-element.58), calls=%async_computation.2 | async-start | bytes 4194304 | tf_op jit(solution)/shard_map/all_to_all | solution.py:252
  117.6 1238.3 %reduce-scatter.11.cloned.1.call-start = ((), (), s32[]{:S(2)}) async-start(), calls=%async_computation.16 | async-start | bytes 2359296 | tf_op jit(solution)/shard_map/reduce_scatter | solution.py:301
  234.8 0.8 copy-start.25
  244.2 6.6 copy-start.6
  259.0 3.7 copy-start.2
  259.9 3.6 copy-start.5
  270.6 1.7 copy-start.8
  678.3 13.5 copy-start.9
  678.3 13.5 copy-start.35
  691.8 11.3 copy-start.13
  703.1 3.2 copy-start.17
  704.7 1.6 copy-start.3
  709.5 646.5 %reduce-scatter.9.cloned.1.call-start = ((), (), s32[]{:S(2)}) async-start(), calls=%async_computation.15 | async-start | bytes 7077888 | tf_op jit(solution)/shard_map/reduce_scatter | solution.py:295
  719.6 7.3 copy-start.20
  723.8 3.1 copy-start.16
  726.9 1.1 copy-start.19
  736.2 1.4 copy-start.18
  736.2 619.8 %reduce-scatter.13.cloned.1.call-start = ((), (), s32[]{:S(2)}) async-start(), calls=%async_computation.17 | async-start | bytes 10616832 | tf_op jit(solution)/shard_map/reduce_scatter | solution.py:307
  750.7 739.1 %reduce-scatter.15.cloned.1.call-start = ((), (), s32[]{:S(2)}) async-start(), calls=%async_computation.18 | async-start | bytes 10616832 | tf_op jit(solution)/shard_map/reduce_scatter | solution.py:310
  763.7 1.3 copy-start.15
  763.7 1.8 copy-start.14
  763.7 892.1 %reduce-scatter.17.cloned.1.call-start = ((), (), s32[]{:S(2)}) async-start(), calls=%async_computation.19 | async-start | bytes 10616832 | tf_op jit(solution)/shard_map/reduce_scatter | solution.py:313
  764.9 33.5 %collective-permute-start = (bf16[576,1024]{1,0:T(8,128)(2,1)S(1)}, bf16[576,1024]{1,0:T(8,128)(2,1)}, u32[]{:S(2)}, u32[]{:S(2)}) collective-permute-start(bf16[576,1024]{1,0:T(8,128)(2,1)S(1)} %copy-done.15), channel_id=1, source_target_pairs={{0,1},{1,0},{2,3},{3,2},{4,5},{5,4},{6,7},{7,6},{8,9},{9,8},{10,11... | collective-permute-start | bytes 3538952 | tf_op jit(solution)/shard_map/ppermute | solution.py:15
  801.7 87.6 %collective-permute-start.1 = (bf16[1152,1024]{1,0:T(8,128)(2,1)}, bf16[1152,1024]{1,0:T(8,128)(2,1)}, u32[]{:S(2)}, u32[]{:S(2)}) collective-permute-start(bf16[1152,1024]{1,0:T(8,128)(2,1)} %maximum_select_fusion.3), channel_id=1, source_target_pairs={{0,2},{1,3},{2,0},{3,1},{4,6},{5,7},{6,4},{7,5},{8,10},{9,11},{10,... | collective-permute-start | bytes 7077896 | tf_op jit(solution)/shard_map/ppermute | solution.py:15
  801.7 96.3 %copy-start.26 = (s32[2]{0:T(128)S(1)}, s32[2]{0:T(128)}, u32[]{:S(2)}) copy-start(s32[2]{0:T(128)} %copy-done.25) | copy-start | bytes 28
  801.7 96.3 %copy-start.28 = (s32[2]{0:T(128)S(1)}, s32[2]{0:T(128)}, u32[]{:S(2)}) copy-start(s32[2]{0:T(128)} %get-tuple-element.60) | copy-start | bytes 28
  895.6 307.4 %collective-permute-start.2 = (bf16[2304,1024]{1,0:T(8,128)(2,1)}, bf16[2304,1024]{1,0:T(8,128)(2,1)}, u32[]{:S(2)}, u32[]{:S(2)}) collective-permute-start(bf16[2304,1024]{1,0:T(8,128)(2,1)} %maximum_select_fusion.2), channel_id=1, source_target_pairs={{0,4},{1,5},{2,6},{3,7},{4,0},{5,1},{6,2},{7,3},{8,12},{9,13},{10,... | collective-permute-start | bytes 14155784 | tf_op jit(solution)/shard_map/ppermute | solution.py:15
  1222.5 10.0 copy-start.4
  1222.5 10.0 copy-start.7
  1245.8 105.3 %all-to-all-start.1 = ((bf16[2,512,1024]{2,0,1:T(2,128)(2,1)}), bf16[2,512,1024]{2,0,1:T(2,128)(2,1)}, u32[]{:S(2)}, u32[]{:S(2)}) async-start(bf16[2,512,1024]{2,0,1:T(2,128)(2,1)} %copy.39), calls=%async_computation.1 | async-start | bytes 4194304 | tf_op jit(solution)/shard_map/all_to_all | solution.py:270
  1351.2 380.7 %all-to-all-start.3 = ((bf16[2,512,1024]{2,0,1:T(2,128)(2,1)}), bf16[2,512,1024]{2,0,1:T(2,128)(2,1)S(1)}, u32[]{:S(2)}, u32[]{:S(2)}) async-start(bf16[2,512,1024]{2,0,1:T(2,128)(2,1)} %copy.43), calls=%async_computation.3 | async-start | bytes 4194304 | tf_op jit(solution)/shard_map/all_to_all | solution.py:289
  1354.8 301.0 %copy-start.34 = (u32[32]{0:T(128)S(1)}, u32[32]{0:T(128)}, u32[]{:S(2)}) copy-start(u32[32]{0:T(128)} %constant.111) | copy-start | bytes 388
  1354.8 302.2 %copy-start.33 = (s32[1,16]{1,0:T(1,128)S(1)}, s32[1,16]{1,0:T(1,128)}, u32[]{:S(2)}) copy-start(s32[1,16]{1,0:T(1,128)} %param.21) | copy-start | bytes 196
  1354.8 365.3 %reduce-scatter.19.cloned.1.call-start = ((), (), s32[]{:S(2)}) async-start(), calls=%async_computation.20 | async-start | bytes 294912
  1355.8 458.5 %all-reduce.11.cloned.1.call-start = ((), (), s32[]{:S(2)}) async-start(), calls=%async_computation.21 | async-start | bytes 9175040 | tf_op jit(solution)/shard_map/psum | solution.py:319
  1732.5 2.4 copy-start.10
  1736.9 3.7 copy-start.11
  1814.3 3.1 copy-start.22
  1814.3 4.7 copy-start.21
  1817.4 3.3 copy-start.23
  1819.0 3.0 copy-start.24
  1819.0 3.8 copy-start.1
Sparse Core Ops, SparseCore 0:
  10.2 174.4 all-gather.7
  186.8 48.0 all-gather.9
  237.1 136.5 all-gather.11
  375.8 136.2 all-gather.13
  514.1 136.2 all-gather.15
  709.6 66.4 reduce-scatter.10
  779.7 259.5 reduce-scatter.8
  1042.8 201.0 reduce-scatter.12
  1247.5 242.1 reduce-scatter.14
  1493.2 162.5 reduce-scatter.16
  1659.7 60.3 reduce-scatter.18
  1722.7 91.6 all-reduce.10
